TPU v7x, 128 devices: a whole 4x4x4 slice. The times are simulated.
128 devices in a mesh: sector: 4 (over y_hi, core), owner: 32 (over x, y_lo, z).
Axes of the slice: x: 4, y: 4 (y_hi: 2, y_lo: 2; y = y_hi * 2 + y_lo), z: 4, core: 2. Of those that a mesh axis runs over, the one named last changes fastest.
Arguments:
- broadcast_ops: float32 [4, 4, 1024, 1024], P('sector', None, 'owner'), may hold values from -0.1875 to 0.1875
- resident_ops: float32 [4, 32, 1024, 1024], P('sector', 'owner'), may hold values from -6 to 6
- integrals: float32 [4, 32, 4, 4], P('sector', 'owner'), may hold values from -3 to 3
- owner_list: int32 [32, 4], P('owner'), may hold values from 0 to 3, as said below
Outputs:
- complementary: float32 [4, 32, 2, 1024, 1024], P('sector', 'owner')
Inputs may be any that keep to these rules, and one draw needn't show every extreme that they name: `owner_list`: in each row one sector group is named exactly 2 times, one is not named, and every other is named once.
All inputs are finite; a program needn't handle non-finite values.
Results may differ from a plain program's by a relative error of at most 0.012.
Values may be sent and summed in bfloat16 or wider, within the bound.
A program may use at most 64 MiB of HBM per device.

v0:
```python
import jax
import jax.numpy as jnp
from jax import lax
from jax.sharding import PartitionSpec as P

CAP = 2


def shards(broadcast_ops, resident_ops, integrals, owner_list):
    highest = lax.Precision.HIGHEST
    shared = broadcast_ops[0]
    resident = resident_ops[0, 0]
    weights = integrals[0, 0]
    owners = owner_list[0]
    pair_count = owners.shape[0]
    slot_count = CAP
    sector_id = lax.axis_index("sector")
    products = jnp.einsum(
        "krj,jn->krn",
        lax.all_gather(shared.astype(jnp.bfloat16), "owner", axis=1, tiled=True).astype(
            jnp.float32
        ),
        resident,
        precision=highest,
    )
    pair_index = jnp.arange(pair_count)
    same_owner = owners[:, None] == owners[None, :]
    earlier = pair_index[:, None] < pair_index[None, :]
    slot_rank = jnp.sum((same_owner & earlier).astype(jnp.int32), axis=0)
    partial_ops = jnp.einsum("pk,kmn->pmn", weights, products, precision=highest)
    pair_total = lax.psum(partial_ops.astype(jnp.bfloat16), "sector").astype(jnp.float32)
    selector = (
        (owners[None, :] == sector_id) & (slot_rank[None, :] == jnp.arange(slot_count)[:, None])
    ).astype(jnp.float32)
    result = jnp.einsum("cp,pmn->cmn", selector, pair_total, precision=highest)
    return result[None, None]


def solution(mesh):
    in_specs = (
        P("sector", None, "owner", None),
        P("sector", "owner", None, None),
        P("sector", "owner", None, None),
        P("owner", None),
    )
    out_specs = P("sector", "owner", None, None, None)
    return jax.shard_map(shards, mesh=mesh, in_specs=in_specs, out_specs=out_specs, check_vma=False)
```

profile of v0, /device:TPU:1, one launch (start us, length us, event | category | flops | bytes accessed | tf_op | source)
XLA Modules:
  0.0 435.2 jit_solution(6021242355717869884)
XLA Ops:
  6.5 0.0 copy-start
  6.5 0.0 all-gather.3.cloned.1.call-start
  6.5 1.8 convert_element_type.19
  8.3 0.0 all-gather.3.cloned.1.call-update
  8.4 0.0 all-reduce.2.cloned.1.call-start
  8.4 149.4 %all-gather.3.cloned.1.call-done = bf16[1,4,1024,1024]{3,2,1,0:T(8,128)(2,1)} async-done(((bf16[1,4,32,1024]{3,2,1,0:T(8,128)(2,1)}), bf16[1,4,1024,1024]{3,2,1,0:T(8,128)(2,1)}) %all-gather.3.cloned.1.call-update) | async-done | bytes 8388624 | tf_op jit(solution)/shard_map/all_gather | solution.py:20
  157.8 31.4 %fusion.2 = f32[4,1024,1024]{2,1,0:T(8,128)S(1)} fusion(bf16[1,4,1024,1024]{3,2,1,0:T(8,128)(2,1)} %all-gather.3.cloned.1.call-done, f32[1,1,1024,1024]{3,2,1,0:T(8,128)} %param.5), kind=kOutput, calls=%fused_computation.2 | convolution fusion | flops 51539607552 | bytes 29360128 | tf_op jit(solution)/shard_map/krj,jn->krn/dot_general | solution.py:18
  189.2 0.0 copy-done
  189.2 44.7 %convert_bitcast_fusion = bf16[4,1024,1024]{2,0,1:T(4,128)(2,1)} fusion(f32[4,1024,1024]{2,1,0:T(8,128)S(1)} %fusion.2, f32[1,1,4,4]{3,2,1,0:T(4,128)S(1)} %copy-done), kind=kOutput, calls=%fused_computation.4 | convolution fusion | flops 205520896 | bytes 25165888 | tf_op jit(solution)/shard_map/pk,kmn->pmn/dot_general | solution.py:30
  233.9 0.0 copy-start.1
  233.9 0.0 all-reduce.2.cloned.1.call-update
  233.9 0.6 copy-done.1
  234.6 0.1 convert_reduce_fusion
  234.7 180.7 %all-reduce.2.cloned.1.call-done = bf16[4,1024,1024]{2,0,1:T(4,128)(2,1)} async-done(((bf16[4,1024,1024]{2,0,1:T(4,128)(2,1)}), bf16[4,1024,1024]{2,0,1:T(4,128)(2,1)}) %all-reduce.2.cloned.1.call-update) | async-done | bytes 8388624 | tf_op jit(solution)/shard_map/psum | solution.py:31
  415.4 7.0 %convolution_bitcast_fusion = f32[1,1,2,1024,1024]{4,2,3,1,0:T(2,128)S(1)} fusion(bf16[4,1024,1024]{2,0,1:T(4,128)(2,1)} %all-reduce.2.cloned.1.call-done, pred[4]{0:T(512)(128)(4,1)S(1)} %compare_bitcast_fusion, s32[4]{0:T(128)S(1)} %convert_reduce_fusion), kind=kOutput, calls=%fused_computation.5 | convolution fusion | flops 16777232 | bytes 16777236 | tf_op jit(solution)/shard_map/cp,pmn->cmn/dot_general | solution.py:35
  422.4 6.0 %copy.6 = f32[1,1,2,1024,1024]{4,3,2,1,0:T(8,128)} copy(f32[1,1,2,1024,1024]{4,2,3,1,0:T(2,128)S(1)} %convolution_bitcast_fusion) | data formatting | bytes 16777216 | tf_op jit(solution)/shard_map/broadcast_in_dim | solution.py:36
  (1 shorter events, 0.0 us)
Async XLA Ops:
  6.5 182.6 %copy-start = (f32[1,1,4,4]{3,2,1,0:T(4,128)S(1)}, f32[1,1,4,4]{3,2,1,0:T(4,128)}, u32[]{:S(2)}) copy-start(f32[1,1,4,4]{3,2,1,0:T(4,128)} %param.6) | copy-start | bytes 196
  6.5 151.2 %all-gather.3.cloned.1.call-start = ((), (), s32[]{:S(2)}) async-start(), calls=%async_computation.1 | async-start | bytes 8650752 | tf_op jit(solution)/shard_map/all_gather | solution.py:20
  8.4 407.0 %all-reduce.2.cloned.1.call-start = ((), (), s32[]{:S(2)}) async-start(), calls=%async_computation | async-start | bytes 16777216 | tf_op jit(solution)/shard_map/psum | solution.py:31
  233.9 0.7 copy-start.1
Sparse Core Ops, SparseCore 0:
  9.0 148.7 all-gather.2
  234.1 181.2 all-reduce.1
where the time goes:
time: 435 us
  waiting for transfers between devices  330 us (76%)
  matrix products  83.2 us (19%)
  between operations  13.4 us (3%)
  local copies, waits for them, and re-layouts  6.59 us (2%)
    psum x1, waiting for transfers between devices, shards(): lax.psum(partial_ops.astype(jnp.bfloat16), 'sector').astype(jnp.float32)  181 us
    all_gather x1, waiting for transfers between devices, shards(): lax.all_gather(shared.astype(jnp.bfloat16), 'owner', axis=1, tiled=True)  149 us
    dot_general x1, matrix products, shards(): jnp.einsum('pk,kmn->pmn', weights, products, precision=highest)  44.7 us
    dot_general x1, matrix products, shards(): jnp.einsum('krj,jn->krn', lax.all_gather(shared.astype(jnp.bfloat16), 'ow...  31.4 us
  transfers between devices with their start and end apart: 2, of which 2 were waited for; matrix products, arithmetic and copies ran while one was open for 0% of the time, Pallas kernels for 0%

commit v1 on v0

--- a/solution.py
+++ b/solution.py
@@ -17,9 +17,12 @@
     sector_id = lax.axis_index("sector")
     products = jnp.einsum(
         "krj,jn->krn",
-        lax.all_gather(shared.astype(jnp.bfloat16), "owner", axis=1, tiled=True).astype(
-            jnp.float32
-        ),
+        jnp.concatenate(
+            lax.all_to_all(
+                jnp.stack([shared.astype(jnp.bfloat16)] * lax.axis_size("owner")), "owner", 0, 0
+            ),
+            axis=1,
+        ).astype(jnp.float32),
         resident,
         precision=highest,
     )

time: 435 us -> 377 us (0.87)
  waiting for transfers between devices: 330 us -> 161 us
  blocking collectives: 0 us -> 103 us
  local copies, waits for them, and re-layouts: 6.59 us -> 16.4 us
    all_gather x1 -> x0, waiting for transfers between devices: 149 us -> none  [shards(): lax.all_gather(shared.astype(jnp.bfloat16), 'owner', axis=1, tiled=True)]
    all_to_all x0 -> x1, blocking collectives: none -> 103 us  [shards(): lax.all_to_all(jnp.stack([shared.astype(jnp.bfloat16)] * lax.axis_size('o...]
    psum x1, waiting for transfers between devices: 181 us -> 160 us  [shards(): lax.psum(partial_ops.astype(jnp.bfloat16), 'sector').astype(jnp.float32)]
    all_to_all x0 -> x1, local copies, waits for them, and re-layouts: none -> 8.79 us  [shards(): lax.all_to_all(jnp.stack([shared.astype(jnp.bfloat16)] * lax.axis_size('o...]
  transfers between devices with their start and end apart: 2 -> 1, of which waited for: 2 -> 1; matrix products, arithmetic and copies ran while one was open for 0% -> 0% of each run, Pallas kernels for 0% -> 0%
where the time goes in v1:
time: 377 us
  waiting for transfers between devices  161 us (43%)
  blocking collectives  103 us (27%)
  matrix products  81.9 us (22%)
  local copies, waits for them, and re-layouts  16.4 us (4%)
  between operations  13.4 us (4%)
    psum x1, waiting for transfers between devices, shards(): lax.psum(partial_ops.astype(jnp.bfloat16), 'sector').astype(jnp.float32)  160 us
    all_to_all x1, blocking collectives, shards(): lax.all_to_all(jnp.stack([shared.astype(jnp.bfloat16)] * lax.axis_size('o...  103 us
    dot_general x1, matrix products, shards(): jnp.einsum('pk,kmn->pmn', weights, products, precision=highest)  44.7 us
    dot_general x1, matrix products, shards(): jnp.einsum('krj,jn->krn', jnp.concatenate(lax.all_to_all(jnp.stack([share...  30.2 us
    all_to_all x1, local copies, waits for them, and re-layouts, shards(): lax.all_to_all(jnp.stack([shared.astype(jnp.bfloat16)] * lax.axis_size('o...  8.79 us
  transfers between devices with their start and end apart: 1, of which 1 were waited for; matrix products, arithmetic and copies ran while one was open for 0% of the time, Pallas kernels for 0%

profile of v1, /device:TPU:1, one launch (start us, length us, event | category | flops | bytes accessed | tf_op | source)
XLA Modules:
  0.0 376.7 jit_solution(14369492109656285635)
XLA Ops:
  6.5 0.0 copy-start
  6.5 0.0 all-reduce.2.cloned.1.call-start
  6.5 1.1 convert_bitcast_fusion.1
  7.6 1.1 stack.5
  8.7 103.2 %all_to_all.5 = bf16[32,4,32,1024]{3,2,1,0:T(8,128)(2,1)} all-to-all(bf16[32,4,32,1024]{3,2,1,0:T(8,128)(2,1)S(1)} %stack.5), channel_id=1, replica_groups=mesh['sector'=4,'owner'=32] {'owner'}, dimensions={0} | all-to-all | bytes 16777216 | tf_op jit(solution)/shard_map/all_to_all | solution.py:21
  111.9 0.0 copy-start.1
  111.9 8.8 %copy.10 = bf16[32,4,32,1024]{3,2,0,1:T(8,128)(2,1)} copy(bf16[32,4,32,1024]{3,2,1,0:T(8,128)(2,1)} %all_to_all.5) | data formatting | bytes 16777216 | tf_op jit(solution)/shard_map/all_to_all | solution.py:21
  120.7 0.0 copy-done.1
  120.7 30.2 %fusion.4 = f32[4,1024,1024]{2,1,0:T(8,128)S(1)} fusion(bf16[4,1024,1024]{2,1,0:T(8,128)(2,1)} %bitcast.27, f32[1,1,1024,1024]{3,2,1,0:T(8,128)S(1)} %copy-done.1), kind=kOutput, calls=%fused_computation.4 | convolution fusion | flops 51539607552 | bytes 29360128 | tf_op jit(solution)/shard_map/krj,jn->krn/dot_general | solution.py:18
  150.9 0.0 copy-done
  150.9 44.7 %convert_bitcast_fusion = bf16[4,1024,1024]{2,0,1:T(4,128)(2,1)} fusion(f32[4,1024,1024]{2,1,0:T(8,128)S(1)} %fusion.4, f32[1,1,4,4]{3,2,1,0:T(4,128)S(1)} %copy-done), kind=kOutput, calls=%fused_computation.2 | convolution fusion | flops 205520896 | bytes 25165888 | tf_op jit(solution)/shard_map/pk,kmn->pmn/dot_general | solution.py:33
  195.7 0.0 copy-start.2
  195.7 0.0 all-reduce.2.cloned.1.call-update
  195.7 0.6 copy-done.2
  196.3 0.1 convert_reduce_fusion
  196.4 160.5 %all-reduce.2.cloned.1.call-done = bf16[4,1024,1024]{2,0,1:T(4,128)(2,1)} async-done(((bf16[4,1024,1024]{2,0,1:T(4,128)(2,1)}), bf16[4,1024,1024]{2,0,1:T(4,128)(2,1)}) %all-reduce.2.cloned.1.call-update) | async-done | bytes 8388624 | tf_op jit(solution)/shard_map/psum | solution.py:34
  356.9 7.0 %convolution_bitcast_fusion = f32[1,1,2,1024,1024]{4,2,3,1,0:T(2,128)S(1)} fusion(bf16[4,1024,1024]{2,0,1:T(4,128)(2,1)} %all-reduce.2.cloned.1.call-done, pred[4]{0:T(512)(128)(4,1)S(1)} %compare_bitcast_fusion, s32[4]{0:T(128)S(1)} %convert_reduce_fusion), kind=kOutput, calls=%fused_computation.3 | convolution fusion | flops 16777232 | bytes 16777236 | tf_op jit(solution)/shard_map/cp,pmn->cmn/dot_general | solution.py:38
  363.9 6.0 %copy.12 = f32[1,1,2,1024,1024]{4,3,2,1,0:T(8,128)} copy(f32[1,1,2,1024,1024]{4,2,3,1,0:T(2,128)S(1)} %convolution_bitcast_fusion) | data formatting | bytes 16777216 | tf_op jit(solution)/shard_map/broadcast_in_dim | solution.py:39
  (1 shorter events, 0.0 us)
Async XLA Ops:
  6.5 144.4 %copy-start = (f32[1,1,4,4]{3,2,1,0:T(4,128)S(1)}, f32[1,1,4,4]{3,2,1,0:T(4,128)}, u32[]{:S(2)}) copy-start(f32[1,1,4,4]{3,2,1,0:T(4,128)} %param.6) | copy-start | bytes 196
  6.5 350.4 %all-reduce.2.cloned.1.call-start = ((), (), s32[]{:S(2)}) async-start(), calls=%async_computation.1 | async-start | bytes 16777216 | tf_op jit(solution)/shard_map/psum | solution.py:34
  111.9 8.8 %copy-start.1 = (f32[1,1,1024,1024]{3,2,1,0:T(8,128)S(1)}, f32[1,1,1024,1024]{3,2,1,0:T(8,128)}, u32[]{:S(2)}) copy-start(f32[1,1,1024,1024]{3,2,1,0:T(8,128)} %param.5) | copy-start | bytes 12582916
  195.7 0.7 copy-start.2
Sparse Core Ops, SparseCore 0:
  195.8 161.0 all-reduce.1
